TPU v7x, 512 devices: a whole 4x8x8 slice. The times are simulated.
512 devices in a mesh: dp: 16 (over z, core), tp: 32 (over y, x).
Axes of the slice: x: 4, y: 8, z: 8, core: 2. Of those that a mesh axis runs over, the one named last changes fastest.
Arguments:
- q_new: bfloat16 [512, 1536], P(('dp', 'tp'))
- new_key_value: bfloat16 [512, 512], P(('dp', 'tp')), may hold values from -6 to 6
- resid_dec: bfloat16 [512, 1536], P(('dp', 'tp')), may hold values from -6 to 6
- placing: int32 [512], replicated, may hold values from 0 to 511, as said below
- lengths: int32 [512], P('dp'), may hold values from 5 to 2048, as said below
- write_pos: int32 [512], P('dp'), may hold values from 4 to 2047, as said below
- k_cache: bfloat16 [512, 2, 2048, 128], P('dp', None, 'tp')
- value_cache: bfloat16 [512, 2, 2048, 128], P('dp', None, 'tp'), may hold values from -6 to 6
- w_out: bfloat16 [1536, 1536], P(None, 'tp'), may hold values from -0.15625 to 0.15625
- x_pre: bfloat16 [32256, 1536], P(('dp', 'tp')), may hold values from -6 to 6
- routes: int32 [32768, 4], P(('dp', 'tp')), may hold values from 0 to 31, all different within a row; in each aligned block of 64 rows (0 to 63, 64 to 127, ...) at most 16 rows name the same one
- route_scale: float32 [32768, 4], P(('dp', 'tp')), may hold values from 0.2 to 2
- moe_gain: float32 [1536], replicated, may hold values from 0.5 to 1.5
- w_gate: bfloat16 [32, 768, 1536], P('tp', 'dp'), may hold values from -0.15625 to 0.15625
- w_up: bfloat16 [32, 768, 1536], P('tp', 'dp'), may hold values from -0.15625 to 0.15625
- w_down: bfloat16 [32, 768, 1536], P('tp', 'dp'), may hold values from -0.21875 to 0.21875
Outputs:
- out_pre: bfloat16 [32256, 1536], P(('dp', 'tp'))
- out_dec: bfloat16 [512, 1536], P(('dp', 'tp'))
Inputs may be any that keep to these rules, and one draw needn't show every extreme that they name: Each of 0 to 511 appears once; cache row j belongs to request placing[j]. `lengths`: a cache row is either full (2048 live slots) or filled from slot 0 up; some row is full. `write_pos`: below the row's length; a row that is not full writes at its length - 1, a full row anywhere past the sink slots. `routes`: the 64 rows of one device name any one expert at most 16 times.
All inputs are finite; a program needn't handle non-finite values.
Results may differ from a plain program's by a relative error of at most 0.007.
Values may be sent and summed in bfloat16 or wider, within the bound.
No kernel may reach another device: no remote copies, remote signals or barrier semaphores. Data moves between devices by JAX's collectives and lax.ppermute only.
A program may use at most 64 MiB of HBM per device.

v0:
```python
import jax
import jax.numpy as jnp
from jax import lax
from jax.sharding import Mesh
from jax.sharding import PartitionSpec as P

TP = ("y", "x")
F32 = jnp.float32
BF16 = jnp.bfloat16


def contract_rows(left_rows, unit_rows):
    return lax.dot_general(
        left_rows, unit_rows, (((1,), (1,)), ((), ())), preferred_element_type=F32
    )


def swap(blocks, axis_name):
    return lax.all_to_all(blocks, axis_name, split_axis=0, concat_axis=0, tiled=True)


def choose_rows(table, rows):
    return jnp.dot(table.astype(BF16), rows, preferred_element_type=F32).astype(BF16)


def pieces_of(x):
    high = lax.reduce_precision(x, 8, 7)
    middle = lax.reduce_precision(x - high, 8, 7)
    low = lax.reduce_precision(x - high - middle, 8, 7)
    return (high.astype(BF16), middle.astype(BF16), low.astype(BF16))


def rms(rows_f32, gain):
    mean_square = jnp.mean(rows_f32 * rows_f32, axis=-1, keepdims=True)
    return (rows_f32 * lax.rsqrt(mean_square + 1e-06) * gain).astype(BF16)


def sum_and_copy(parts, copies):
    count, rows, columns = parts.shape
    same = jnp.arange(copies * rows, dtype=jnp.int32)[:, None] % rows
    same = same == jnp.arange(count * rows, dtype=jnp.int32)[None, :] % rows
    return choose_rows(same, parts.reshape(count * rows, columns)).reshape(copies, rows, columns)


def expert_units(rows, units, gate):
    upper = contract_rows(rows, units[1])
    active = (jnp.maximum(gate, 0.0) * upper).astype(BF16)
    return jnp.dot(active, units[2], preferred_element_type=F32).astype(BF16)


def on_device(
    q_new,
    new_key_value,
    resid_dec,
    placing,
    lengths,
    write_pos,
    k_cache,
    value_cache,
    w_out,
    x_pre,
    routes,
    route_scale,
    moe_gain,
    w_gate,
    w_up,
    w_down,
):
    dp_size = lax.axis_size("dp")
    lines, posts = (lax.axis_size("y"), lax.axis_size("x"))
    tp_size = lines * posts
    dp_group = lax.axis_index("dp")
    line = lax.axis_index("y")
    tp_lane = line * posts + lax.axis_index("x")
    group_reqs, kv_heads, slot_dev, head_size = k_cache.shape
    width = q_new.shape[1]
    heads = width // head_size
    per_group = heads // kv_heads
    total_reqs = placing.shape[0]
    experts = tp_size * w_gate.shape[0]
    assert group_reqs == tp_size and experts == tp_size
    no_value = jnp.zeros((), BF16)
    rows_dev, top_count = routes.shape
    pre_rows = rows_dev - 1
    capacity = min(2 * rows_dev * top_count // experts, rows_dev)
    route_weight = route_scale / jnp.sum(route_scale, axis=-1, keepdims=True)
    expert_ids = jnp.arange(experts, dtype=jnp.int32)
    hits = routes[:, :, None] == expert_ids[None, None, :]
    weight_of = jnp.sum(jnp.where(hits, route_weight[:, :, None], 0.0), axis=1)
    routed = jnp.any(hits[:pre_rows], axis=1)
    row_ids = jnp.arange(pre_rows, dtype=jnp.int32)
    before = (row_ids[None, :] < row_ids[:, None]).astype(BF16)
    position = jnp.dot(before, routed.astype(BF16), preferred_element_type=F32).astype(jnp.int32)
    slots = jnp.arange(capacity, dtype=jnp.int32)
    pick = routed[:, :, None] & (position[:, :, None] == slots[None, None, :])
    pick_table = pick.reshape(pre_rows, experts * capacity)
    x_f32 = x_pre.astype(F32)
    outgoing = lax.dot_general(
        pick_table.astype(BF16),
        lax.optimization_barrier(rms(x_f32, moe_gain)),
        (((0,), (0,)), ((), ())),
        preferred_element_type=F32,
    ).astype(BF16)
    stored, outgoing = lax.optimization_barrier(((w_gate, w_up, w_down), outgoing))
    units = lax.all_gather(jnp.concatenate(stored, axis=0), "dp", axis=1, tiled=True)
    columns = heads + 2 * kv_heads
    share = columns * head_size // posts
    post = lax.axis_index("x")
    fresh = jnp.concatenate([q_new, new_key_value], axis=1)
    fresh, outgoing = lax.optimization_barrier((fresh, outgoing))
    received = swap(outgoing.reshape(experts, capacity, width), TP)
    line_fresh = lax.all_gather(fresh, "x", axis=0, tiled=True)
    line_share = lax.dynamic_slice_in_dim(line_fresh, post * share, share, axis=1)
    all_rows = lax.all_gather(line_share, "dp", axis=0, tiled=True)
    wanted = lax.dynamic_slice_in_dim(placing, dp_group * group_reqs, group_reqs)
    held = jnp.arange(dp_size, dtype=jnp.int32)[:, None] * tp_size + line * posts
    held = (held + jnp.arange(posts, dtype=jnp.int32)[None, :]).reshape(1, dp_size * posts)
    mine = choose_rows(jnp.tile(wanted, lines)[:, None] == held, all_rows)
    mine, received = lax.optimization_barrier((mine, received))
    chosen = swap(mine.reshape(lines, group_reqs, share), "y")
    cached = swap(sum_and_copy(chosen, posts), "x").reshape(
        posts, group_reqs, columns // posts, head_size
    )
    cached = jnp.transpose(cached, (1, 0, 2, 3)).reshape(group_reqs, columns, head_size)
    query_head_list = cached[:, :heads].reshape(group_reqs, kv_heads, per_group, head_size)
    incoming_key = cached[:, heads : heads + kv_heads][:, :, None, :]
    incoming_value = cached[:, heads + kv_heads :][:, :, None, :]
    slot_ids = tp_lane * slot_dev + jnp.arange(slot_dev, dtype=jnp.int32)
    written = (slot_ids[None, :] == write_pos[:, None])[:, None, :, None]
    key_rows = jnp.where(written, incoming_key, k_cache)
    value_rows = jnp.where(written, incoming_value, value_cache)
    scores = jnp.einsum(
        "rgqd,rgsd->rgqs", query_head_list, key_rows, preferred_element_type=F32
    ) * head_size ** (-0.5)
    is_valid = (slot_ids[None, :] < lengths[:, None])[:, None, None, :]
    masked = jnp.where(is_valid, scores, -1e30)
    local_peak = jnp.max(masked, axis=-1)
    weights = jnp.where(is_valid, jnp.exp(masked - local_peak[..., None]), 0.0)
    local_total = jnp.sum(weights, axis=-1)
    high = lax.reduce_precision(weights, 8, 7)
    halves = jnp.concatenate([high, weights - high], axis=2).astype(BF16)
    local_mixed = jnp.einsum("rgqs,rgsd->rgqd", halves, value_rows, preferred_element_type=F32)
    local_mixed = local_mixed[:, :, :per_group] + local_mixed[:, :, per_group:]

    def lane_row(values):
        row = jnp.concatenate(pieces_of(values.reshape(group_reqs, heads)), axis=1)
        return jnp.pad(row, ((0, 0), (0, head_size - row.shape[1])))[:, None, :]

    parts = jnp.concatenate(
        [
            local_mixed.reshape(group_reqs, heads, head_size).astype(BF16),
            lane_row(local_peak),
            lane_row(local_total),
            jnp.zeros((group_reqs, 2, head_size), BF16),
        ],
        axis=1,
    )
    gathered = swap(parts, TP)
    arrived = received.reshape(experts * capacity, width)
    gathered, gate = lax.optimization_barrier((gathered, contract_rows(arrived, units[0])))
    tail = gathered[:, heads : heads + 2, : 3 * heads].astype(F32)
    tail = tail[..., :heads] + tail[..., heads : 2 * heads] + tail[..., 2 * heads :]
    peaks, totals = (tail[:, 0], tail[:, 1])
    scale = jnp.exp(peaks - jnp.max(peaks, axis=0, keepdims=True))
    total = jnp.sum(scale * totals, axis=0)
    mixed = jnp.sum(scale[:, :, None] * gathered[:, :heads].astype(F32), axis=0)
    attention_row = (mixed / total[:, None]).astype(BF16)
    rows = jnp.concatenate([attention_row, resid_dec.reshape(heads, head_size)], axis=0)
    group_rows = swap(jnp.broadcast_to(rows[None], (tp_size,) + rows.shape), TP)
    pre_out = expert_units(arrived, units, gate)
    group_rows, pre_out = lax.optimization_barrier((group_rows, pre_out))
    returned = swap(pre_out.reshape(experts, capacity, width), TP)
    attention = group_rows[:, :heads].reshape(group_reqs, width)
    resid_rows = group_rows[:, heads:].reshape(group_reqs, width)
    projected = jnp.dot(attention, w_out, preferred_element_type=F32).astype(BF16)
    all_projected = lax.all_gather(projected, "dp", axis=0, tiled=True)
    home_ids = dp_group * group_reqs + jnp.arange(group_reqs, dtype=jnp.int32)
    at_home = choose_rows(home_ids[:, None] == placing[None, :], all_projected)
    at_home, returned = lax.optimization_barrier((at_home, returned))
    packed = at_home.reshape(heads, head_size)
    packed = swap(jnp.broadcast_to(packed[None], (tp_size,) + packed.shape), TP)
    proj_home = packed.reshape(tp_size, group_reqs, width // tp_size)
    proj_home = jnp.transpose(proj_home, (1, 0, 2)).reshape(group_reqs, width)
    proj_home = lax.optimization_barrier(proj_home)
    hidden_all = (resid_rows.astype(F32) + proj_home.astype(F32)).astype(BF16)
    own_row = lax.dynamic_slice_in_dim(hidden_all, tp_lane, 1)
    normed_dec = rms(hidden_all.astype(F32), moe_gain)
    dec_out = expert_units(normed_dec, units, contract_rows(normed_dec, units[0]))
    own_row, dec_out = lax.optimization_barrier((own_row, dec_out))
    dec_back = swap(dec_out.reshape(group_reqs, heads, head_size), TP).astype(F32)
    dec_weight = weight_of[pre_rows:].reshape(experts, 1, 1)
    dec_mixture = jnp.sum(dec_weight * dec_back, axis=0).reshape(1, width)
    out_dec = (own_row.astype(F32) + dec_mixture).astype(BF16)
    flat_back = returned.reshape(experts * capacity, width)
    high, middle, low = pieces_of(weight_of[:pre_rows])

    def mix(piece):
        table = jnp.where(pick, piece[:, :, None], no_value)
        return jnp.dot(
            table.reshape(pre_rows, experts * capacity), flat_back, preferred_element_type=F32
        )

    out_pre = (x_f32 + (mix(high) + mix(middle) + mix(low))).astype(BF16)
    return (out_pre, out_dec)


def solution(mesh):
    groups, lanes = mesh.devices.shape
    lines = min(8, groups)
    fine = Mesh(mesh.devices.reshape(groups, lines, lanes // lines), ("dp", "y", "x"))
    rows = P(("dp", "y", "x"), None)
    units = P(TP, "dp", None)
    cache = P("dp", None, TP, None)
    placed = (rows, rows, rows, P(), P("dp"), P("dp"), cache, cache, P(None, TP))
    placed = placed + (rows, rows, rows, P(), units, units, units)
    return jax.shard_map(
        on_device, mesh=fine, in_specs=placed, out_specs=(rows, rows), check_vma=False
    )
```

profile of v0, /device:TPU:8, one launch (start us, length us, event | category | flops | bytes accessed | tf_op | source)
XLA Modules:
  0.0 216.4 jit_solution(434798193457296705)
XLA Ops:
  10.6 1.8 convolution_convert_fusion.1
  13.3 10.2 %all-to-all-start = ((bf16[32,16,1536]{2,1,0:T(8,128)(2,1)}), bf16[32,16,1536]{2,1,0:T(8,128)(2,1)S(1)}, u32[]{:S(2)}, u32[]{:S(2)}) async-start(bf16[32,16,1536]{2,1,0:T(8,128)(2,1)} %bitcast.3), calls=%async_computation | async-start | bytes 3145728 | tf_op jit(solution)/shard_map/all_to_all | solution.py:19
  23.6 12.4 %all-gather = bf16[4,1,2048]{2,1,0:T(2,128)(2,1)S(1)} all-gather(bf16[1,1,2048]{2,1,0:T(2,128)(2,1)S(1)} %bitcast.119), channel_id=1, replica_groups=mesh['dp'=16,'y'=8,'x'=4] {'x'}, dimensions={0}, use_global_device_ids=true | all-gather | bytes 20480 | tf_op jit(solution)/shard_map/all_gather | solution.py:112
  36.0 23.4 %all-gather.1 = bf16[16,4,512]{2,1,0:T(4,128)(2,1)S(1)} all-gather(bf16[1,4,512]{2,1,0:T(4,128)(2,1)S(1)} %bitcast.121), channel_id=1, replica_groups=mesh['dp'=16,'y'=8,'x'=4] {'dp'}, dimensions={0}, use_global_device_ids=true | all-gather | bytes 69632 | tf_op jit(solution)/shard_map/all_gather | solution.py:114
  61.9 8.0 %all-to-all-start.1 = ((bf16[8,32,512]{2,1,0:T(8,128)(2,1)}), bf16[8,32,512]{2,1,0:T(8,128)(2,1)S(1)}, u32[]{:S(2)}, u32[]{:S(2)}) async-start(bf16[8,32,512]{2,1,0:T(8,128)(2,1)} %bitcast.4), calls=%async_computation.1 | async-start | bytes 524288 | tf_op jit(solution)/shard_map/all_to_all | solution.py:19
  69.9 10.9 %all-to-all-done.1 = bf16[8,32,512]{2,1,0:T(8,128)(2,1)S(1)} async-done(((bf16[8,32,512]{2,1,0:T(8,128)(2,1)}), bf16[8,32,512]{2,1,0:T(8,128)(2,1)S(1)}, u32[]{:S(2)}, u32[]{:S(2)}) %all-to-all-start.1) | async-done | bytes 262176 | tf_op jit(solution)/shard_map/all_to_all | solution.py:19
  81.7 3.3 %all-to-all-start.2 = ((bf16[4,32,512]{2,1,0:T(8,128)(2,1)}), bf16[4,32,512]{2,1,0:T(8,128)(2,1)S(1)}, u32[]{:S(2)}, u32[]{:S(2)}) async-start(bf16[4,32,512]{2,1,0:T(8,128)(2,1)} %bitcast.6), calls=%async_computation.2 | async-start | bytes 262144 | tf_op jit(solution)/shard_map/all_to_all | solution.py:19
  85.3 5.7 %all-to-all-done.2 = bf16[4,32,512]{2,1,0:T(8,128)(2,1)S(1)} async-done(((bf16[4,32,512]{2,1,0:T(8,128)(2,1)}), bf16[4,32,512]{2,1,0:T(8,128)(2,1)S(1)}, u32[]{:S(2)}, u32[]{:S(2)}) %all-to-all-start.2) | async-done | bytes 131104 | tf_op jit(solution)/shard_map/all_to_all | solution.py:19
  92.6 1.7 fusion.12
  95.6 5.0 %all-to-all-start.3 = ((bf16[32,16,128]{2,1,0:T(8,128)(2,1)}), bf16[32,16,128]{2,1,0:T(8,128)(2,1)S(1)}, u32[]{:S(2)}, u32[]{:S(2)}) async-start(bf16[32,16,128]{2,1,0:T(8,128)(2,1)} %copy.83), calls=%async_computation.3 | async-start | bytes 262144 | tf_op jit(solution)/shard_map/all_to_all | solution.py:19
  100.6 4.3 %fusion.5 = f32[512,768]{1,0:T(8,128)} fusion(bf16[512,1536]{1,0:T(8,128)(2,1)S(1)} %bitcast.106, bf16[3,768,1536]{2,1,0:T(8,128)(2,1)} %all-gather.4.cloned.1.call-done), kind=kOutput, calls=%fused_computation.14 | convolution fusion | flops 1207959552 | bytes 5505024 | tf_op jit(solution)/shard_map/dot_general | solution.py:13
  104.9 5.3 %all-to-all-done.3 = bf16[32,16,128]{2,1,0:T(8,128)(2,1)S(1)} async-done(((bf16[32,16,128]{2,1,0:T(8,128)(2,1)}), bf16[32,16,128]{2,1,0:T(8,128)(2,1)S(1)}, u32[]{:S(2)}, u32[]{:S(2)}) %all-to-all-start.3) | async-done | bytes 131104 | tf_op jit(solution)/shard_map/all_to_all | solution.py:19
  111.4 4.7 %all-to-all-start.4 = ((bf16[32,24,128]{2,1,0:T(8,128)(2,1)}), bf16[32,24,128]{2,1,0:T(8,128)(2,1)S(1)}, u32[]{:S(2)}, u32[]{:S(2)}) async-start(bf16[32,24,128]{2,1,0:T(8,128)(2,1)} %broadcast_in_dim.147), calls=%async_computation.4 | async-start | bytes 393216 | tf_op jit(solution)/shard_map/all_to_all | solution.py:19
  116.1 7.2 %convolution_convert_fusion = bf16[512,1536]{1,0:T(8,128)(2,1)} fusion(bf16[3,768,1536]{2,1,0:T(8,128)(2,1)} %all-gather.4.cloned.1.call-done, f32[512,768]{1,0:T(8,128)} %fusion.5, bf16[512,1536]{1,0:T(8,128)(2,1)S(1)} %bitcast.107), kind=kOutput, calls=%fused_computation | convolution fusion | flops 2417885184 | bytes 9437184 | tf_op jit(solution)/shard_map/dot_general | solution.py:48
  123.4 3.1 %all-to-all-done.4 = bf16[32,24,128]{2,1,0:T(8,128)(2,1)S(1)} async-done(((bf16[32,24,128]{2,1,0:T(8,128)(2,1)}), bf16[32,24,128]{2,1,0:T(8,128)(2,1)S(1)}, u32[]{:S(2)}, u32[]{:S(2)}) %all-to-all-start.4) | async-done | bytes 196640 | tf_op jit(solution)/shard_map/all_to_all | solution.py:19
  126.4 6.9 %all-to-all-start.5 = ((bf16[32,16,1536]{2,1,0:T(8,128)(2,1)}), bf16[32,16,1536]{2,1,0:T(8,128)(2,1)S(1)}, u32[]{:S(2)}, u32[]{:S(2)}) async-start(bf16[32,16,1536]{2,1,0:T(8,128)(2,1)} %bitcast.20), calls=%async_computation.5 | async-start | bytes 3145728 | tf_op jit(solution)/shard_map/all_to_all | solution.py:19
  133.9 20.2 %all_gather.15 = bf16[512,48]{1,0:T(8,128)(2,1)S(1)} all-gather(bf16[32,48]{1,0:T(8,128)(2,1)S(1)} %convolution_convert_fusion.7), channel_id=1, replica_groups=mesh['dp'=16,'y'=8,'x'=4] {'dp'}, dimensions={0}, use_global_device_ids=true | all-gather | bytes 52224 | tf_op jit(solution)/shard_map/all_gather | solution.py:176
  154.2 15.4 %all-to-all-done.5 = bf16[32,16,1536]{2,1,0:T(8,128)(2,1)S(1)} async-done(((bf16[32,16,1536]{2,1,0:T(8,128)(2,1)}), bf16[32,16,1536]{2,1,0:T(8,128)(2,1)S(1)}, u32[]{:S(2)}, u32[]{:S(2)}) %all-to-all-start.5) | async-done | bytes 1572896 | tf_op jit(solution)/shard_map/all_to_all | solution.py:19
  170.4 6.5 %all-to-all-start.6 = ((bf16[32,12,128]{2,1,0:T(8,128)(2,1)}), bf16[32,12,128]{2,1,0:T(8,128)(2,1)S(1)}, u32[]{:S(2)}, u32[]{:S(2)}) async-start(bf16[32,12,128]{2,1,0:T(8,128)(2,1)} %broadcast_in_dim.151), calls=%async_computation.6 | async-start | bytes 262144 | tf_op jit(solution)/shard_map/all_to_all | solution.py:19
  177.8 8.7 %all-to-all-done.6 = bf16[32,12,128]{2,1,0:T(8,128)(2,1)S(1)} async-done(((bf16[32,12,128]{2,1,0:T(8,128)(2,1)}), bf16[32,12,128]{2,1,0:T(8,128)(2,1)S(1)}, u32[]{:S(2)}, u32[]{:S(2)}) %all-to-all-start.6) | async-done | bytes 98336 | tf_op jit(solution)/shard_map/all_to_all | solution.py:19
  187.4 2.4 %fusion.10 = f32[32,768]{1,0:T(8,128)S(1)} fusion(bf16[3,768,1536]{2,1,0:T(8,128)(2,1)} %all-gather.4.cloned.1.call-done, bf16[32,1536]{1,0:T(8,128)(2,1)S(1)} %get-tuple-element.35, f32[1536]{0:T(1024)S(1)} %copy-done.5, f32[32]{0:T(128)S(1)} %add_rsqrt_fusion), kind=kOutput, calls=%fused_computation.23 | convolution fusion | flops 75718656 | bytes 2562176 | tf_op jit(solution)/shard_map/dot_general | solution.py:13
  189.8 3.9 %convolution_convert_fusion.2 = bf16[32,1536]{1,0:T(8,128)(2,1)S(1)} fusion(bf16[3,768,1536]{2,1,0:T(8,128)(2,1)} %all-gather.4.cloned.1.call-done, f32[32,768]{1,0:T(8,128)S(1)} %fusion.10, bf16[32,1536]{1,0:T(8,128)(2,1)S(1)} %get-tuple-element.35, f32[1536]{0:T(1024)S(1)} %copy-done.5, f32[32]{0:T(128)S(1)} %add_rsqrt_fusion), kind=kOutput, calls=%fused_computation.12 | convolution fusion | flops 151289856 | bytes 5019776 | tf_op jit(solution)/shard_map/dot_general | solution.py:48
  194.5 4.7 %all-to-all-start.7 = ((bf16[32,12,128]{2,1,0:T(8,128)(2,1)}), bf16[32,12,128]{2,1,0:T(8,128)(2,1)S(1)}, u32[]{:S(2)}, u32[]{:S(2)}) async-start(bf16[32,12,128]{2,1,0:T(8,128)(2,1)} %reshape.245), calls=%async_computation.7 | async-start | bytes 262144 | tf_op jit(solution)/shard_map/all_to_all | solution.py:19
  200.3 8.5 %all-to-all-done.7 = bf16[32,12,128]{2,1,0:T(8,128)(2,1)S(1)} async-done(((bf16[32,12,128]{2,1,0:T(8,128)(2,1)}), bf16[32,12,128]{2,1,0:T(8,128)(2,1)S(1)}, u32[]{:S(2)}, u32[]{:S(2)}) %all-to-all-start.7) | async-done | bytes 98336 | tf_op jit(solution)/shard_map/all_to_all | solution.py:19
  (117 shorter events, 17.5 us)
Async XLA Ops:
  7.2 126.5 %copy-start = (bf16[1536,48]{0,1:T(8,128)(2,1)S(1)}, bf16[1536,48]{0,1:T(8,128)(2,1)}, u32[]{:S(2)}) copy-start(bf16[1536,48]{0,1:T(8,128)(2,1)} %param.24) | copy-start | bytes 442372
  7.2 5.2 %copy-start.4 = (bf16[1,48,1536]{2,1,0:T(8,128)(2,1)S(1)}, bf16[1,48,1536]{2,1,0:T(8,128)(2,1)}, u32[]{:S(2)}) copy-start(bf16[1,48,1536]{2,1,0:T(8,128)(2,1)} %param.29) | copy-start | bytes 442372
  7.2 5.2 %copy-start.3 = (bf16[1,48,1536]{2,1,0:T(8,128)(2,1)S(1)}, bf16[1,48,1536]{2,1,0:T(8,128)(2,1)}, u32[]{:S(2)}) copy-start(bf16[1,48,1536]{2,1,0:T(8,128)(2,1)} %param.30) | copy-start | bytes 442372
  7.2 5.2 %copy-start.2 = (bf16[1,48,1536]{2,1,0:T(8,128)(2,1)S(1)}, bf16[1,48,1536]{2,1,0:T(8,128)(2,1)}, u32[]{:S(2)}) copy-start(bf16[1,48,1536]{2,1,0:T(8,128)(2,1)} %param.31) | copy-start | bytes 442372
  7.2 93.4 %all-gather.4.cloned.1.call-start = ((), (), s32[]{:S(2)}) async-start(), calls=%async_computation.8 | async-start | bytes 7520256 | tf_op jit(solution)/shard_map/all_gather | solution.py:105
  10.6 2.7 %copy-start.8 = (bf16[1,1536]{1,0:T(2,128)(2,1)S(1)}, bf16[1,1536]{1,0:T(2,128)(2,1)}, u32[]{:S(2)}) copy-start(bf16[1,1536]{1,0:T(2,128)(2,1)} %param.16) | copy-start | bytes 9220
  10.6 2.7 %copy-start.10 = (bf16[1,512]{1,0:T(2,128)(2,1)S(1)}, bf16[1,512]{1,0:T(2,128)(2,1)}, u32[]{:S(2)}) copy-start(bf16[1,512]{1,0:T(2,128)(2,1)} %param.17) | copy-start | bytes 3076
  13.3 46.1 %copy-start.14 = (s32[512]{0:T(512)S(1)}, s32[512]{0:T(512)}, u32[]{:S(2)}) copy-start(s32[512]{0:T(512)} %param.19) | copy-start | bytes 6148
  13.3 48.6 %all-to-all-start = ((bf16[32,16,1536]{2,1,0:T(8,128)(2,1)}), bf16[32,16,1536]{2,1,0:T(8,128)(2,1)S(1)}, u32[]{:S(2)}, u32[]{:S(2)}) async-start(bf16[32,16,1536]{2,1,0:T(8,128)(2,1)} %bitcast.3), calls=%async_computation | async-start | bytes 3145728 | tf_op jit(solution)/shard_map/all_to_all | solution.py:19
  23.5 61.5 %copy-start.11 = (s32[32]{0:T(128)S(1)}, s32[32]{0:T(128)}, u32[]{:S(2)}) copy-start(s32[32]{0:T(128)} %param.20) | copy-start | bytes 388
  23.5 61.5 %copy-start.12 = (s32[32]{0:T(128)S(1)}, s32[32]{0:T(128)}, u32[]{:S(2)}) copy-start(s32[32]{0:T(128)} %param.21) | copy-start | bytes 388
  23.5 61.7 %copy-start.9 = (bf16[1,1536]{1,0:T(2,128)(2,1)S(1)}, bf16[1,1536]{1,0:T(2,128)(2,1)}, u32[]{:S(2)}) copy-start(bf16[1,1536]{1,0:T(2,128)(2,1)} %param.18) | copy-start | bytes 9220
  23.6 67.5 %copy-start.13 = (bf16[32,2,64,128]{3,2,1,0:T(8,128)(2,1)S(1)}, bf16[32,2,64,128]{3,2,1,0:T(8,128)(2,1)}, u32[]{:S(2)}) copy-start(bf16[32,2,64,128]{3,2,1,0:T(8,128)(2,1)} %param.22) | copy-start | bytes 3145732
  61.9 18.9 %all-to-all-start.1 = ((bf16[8,32,512]{2,1,0:T(8,128)(2,1)}), bf16[8,32,512]{2,1,0:T(8,128)(2,1)S(1)}, u32[]{:S(2)}, u32[]{:S(2)}) async-start(bf16[8,32,512]{2,1,0:T(8,128)(2,1)} %bitcast.4), calls=%async_computation.1 | async-start | bytes 524288 | tf_op jit(solution)/shard_map/all_to_all | solution.py:19
  81.7 9.3 %all-to-all-start.2 = ((bf16[4,32,512]{2,1,0:T(8,128)(2,1)}), bf16[4,32,512]{2,1,0:T(8,128)(2,1)S(1)}, u32[]{:S(2)}, u32[]{:S(2)}) async-start(bf16[4,32,512]{2,1,0:T(8,128)(2,1)} %bitcast.6), calls=%async_computation.2 | async-start | bytes 262144 | tf_op jit(solution)/shard_map/all_to_all | solution.py:19
  95.6 14.6 %all-to-all-start.3 = ((bf16[32,16,128]{2,1,0:T(8,128)(2,1)}), bf16[32,16,128]{2,1,0:T(8,128)(2,1)S(1)}, u32[]{:S(2)}, u32[]{:S(2)}) async-start(bf16[32,16,128]{2,1,0:T(8,128)(2,1)} %copy.83), calls=%async_computation.3 | async-start | bytes 262144 | tf_op jit(solution)/shard_map/all_to_all | solution.py:19
  111.4 15.0 %all-to-all-start.4 = ((bf16[32,24,128]{2,1,0:T(8,128)(2,1)}), bf16[32,24,128]{2,1,0:T(8,128)(2,1)S(1)}, u32[]{:S(2)}, u32[]{:S(2)}) async-start(bf16[32,24,128]{2,1,0:T(8,128)(2,1)} %broadcast_in_dim.147), calls=%async_computation.4 | async-start | bytes 393216 | tf_op jit(solution)/shard_map/all_to_all | solution.py:19
  126.4 7.0 %copy-start.7 = (f32[64,4]{0,1:T(4,128)S(1)}, f32[64,4]{0,1:T(4,128)}, u32[]{:S(2)}) copy-start(f32[64,4]{0,1:T(4,128)} %param.27) | copy-start | bytes 3076
  126.4 7.0 %copy-start.6 = (s32[64,4]{0,1:T(4,128)S(1)}, s32[64,4]{0,1:T(4,128)}, u32[]{:S(2)}) copy-start(s32[64,4]{0,1:T(4,128)} %param.26) | copy-start | bytes 3076
  126.4 43.2 %all-to-all-start.5 = ((bf16[32,16,1536]{2,1,0:T(8,128)(2,1)}), bf16[32,16,1536]{2,1,0:T(8,128)(2,1)S(1)}, u32[]{:S(2)}, u32[]{:S(2)}) async-start(bf16[32,16,1536]{2,1,0:T(8,128)(2,1)} %bitcast.20), calls=%async_computation.5 | async-start | bytes 3145728 | tf_op jit(solution)/shard_map/all_to_all | solution.py:19
  170.4 16.0 %all-to-all-start.6 = ((bf16[32,12,128]{2,1,0:T(8,128)(2,1)}), bf16[32,12,128]{2,1,0:T(8,128)(2,1)S(1)}, u32[]{:S(2)}, u32[]{:S(2)}) async-start(bf16[32,12,128]{2,1,0:T(8,128)(2,1)} %broadcast_in_dim.151), calls=%async_computation.6 | async-start | bytes 262144 | tf_op jit(solution)/shard_map/all_to_all | solution.py:19
  177.3 10.0 %copy-start.5 = (f32[1536]{0:T(1024)S(1)}, f32[1536]{0:T(1024)}, u32[]{:S(2)}) copy-start(f32[1536]{0:T(1024)} %param.28) | copy-start | bytes 18436
  189.8 9.4 %copy-start.1 = (bf16[63,1536]{1,0:T(8,128)(2,1)S(1)}, bf16[63,1536]{1,0:T(8,128)(2,1)}, u32[]{:S(2)}) copy-start(bf16[63,1536]{1,0:T(8,128)(2,1)} %param.25) | copy-start | bytes 580612
  194.5 14.3 %all-to-all-start.7 = ((bf16[32,12,128]{2,1,0:T(8,128)(2,1)}), bf16[32,12,128]{2,1,0:T(8,128)(2,1)S(1)}, u32[]{:S(2)}, u32[]{:S(2)}) async-start(bf16[32,12,128]{2,1,0:T(8,128)(2,1)} %reshape.245), calls=%async_computation.7 | async-start | bytes 262144 | tf_op jit(solution)/shard_map/all_to_all | solution.py:19
Sparse Core Ops, SparseCore 0:
  13.4 58.0 all-gather.3
where the time goes:
time: 217 us; the launch traced here: 216 us
  waiting for transfers between devices  58.8 us (27%)
  blocking collectives  56 us (26%)
  starting transfers between devices  49.3 us (23%)
  matrix products  26.8 us (12%)
  between operations  14.6 us (7%)
  other arithmetic  6.01 us (3%)
  local copies, waits for them, and re-layouts  4.88 us (2%)
    all_to_all x8, waiting for transfers between devices, swap(): lax.all_to_all(blocks, axis_name, split_axis=0, concat_axis=0, tiled=True)  58.7 us
    all_to_all x8, starting transfers between devices, swap(): lax.all_to_all(blocks, axis_name, split_axis=0, concat_axis=0, tiled=True)  49.3 us
    all_gather x1, blocking collectives, on_device(): all_rows = lax.all_gather(line_share, 'dp', axis=0, tiled=True)  23.4 us
    all_gather x1, blocking collectives, on_device(): all_projected = lax.all_gather(projected, 'dp', axis=0, tiled=True)  20.2 us
    all_gather x1, blocking collectives, on_device(): line_fresh = lax.all_gather(fresh, 'x', axis=0, tiled=True)  12.4 us
    dot_general x2, matrix products, expert_units(): return jnp.dot(active, units[2], preferred_element_type=F32).astype(BF16)  11.1 us
    dot_general x2, matrix products, contract_rows(): lax.dot_general(left_rows, unit_rows, (((1,), (1,)), ((), ())), preferred...  6.75 us
  transfers between devices with their start and end apart: 9, of which 8 were waited for; matrix products, arithmetic and copies ran while one was open for 10% of the time, Pallas kernels for 0%

commit v1 on v0

--- a/solution.py
+++ b/solution.py
@@ -173,7 +173,9 @@
     attention = group_rows[:, :heads].reshape(group_reqs, width)
     resid_rows = group_rows[:, heads:].reshape(group_reqs, width)
     projected = jnp.dot(attention, w_out, preferred_element_type=F32).astype(BF16)
-    all_projected = lax.all_gather(projected, "dp", axis=0, tiled=True)
+    all_projected = jnp.concatenate(
+        lax.all_to_all(jnp.stack([projected] * lax.axis_size("dp")), "dp", 0, 0), axis=0
+    )
     home_ids = dp_group * group_reqs + jnp.arange(group_reqs, dtype=jnp.int32)
     at_home = choose_rows(home_ids[:, None] == placing[None, :], all_projected)
     at_home, returned = lax.optimization_barrier((at_home, returned))

time: 217 us -> 235 us (1.083)
  waiting for transfers between devices: 58.8 us -> 81.4 us
  blocking collectives: 56 us -> 50.4 us
    all_to_all x8, waiting for transfers between devices: 58.7 us -> 81.4 us  [swap(): lax.all_to_all(blocks, axis_name, split_axis=0, concat_axis=0, tiled=True)]
    all_gather x1 -> x0, blocking collectives: 20.2 us -> none  [on_device(): all_projected = lax.all_gather(projected, 'dp', axis=0, tiled=True)]
    all_to_all x0 -> x1, blocking collectives: none -> 14.6 us  [on_device(): lax.all_to_all(jnp.stack([projected] * lax.axis_size('dp')), 'dp', 0, 0)]
  transfers between devices with their start and end apart: 9 -> 9, of which waited for: 8 -> 8; matrix products, arithmetic and copies ran while one was open for 10% -> 9% of each run, Pallas kernels for 0% -> 0%
where the time goes in v1:
time: 235 us; the launch traced here: 234 us
  waiting for transfers between devices  81.4 us (35%)
  blocking collectives  50.4 us (21%)
  starting transfers between devices  49.5 us (21%)
  matrix products  26.8 us (11%)
  between operations  14.6 us (6%)
  other arithmetic  6.02 us (3%)
  local copies, waits for them, and re-layouts  5.26 us (2%)
    all_to_all x8, waiting for transfers between devices, swap(): lax.all_to_all(blocks, axis_name, split_axis=0, concat_axis=0, tiled=True)  81.4 us
    all_to_all x8, starting transfers between devices, swap(): lax.all_to_all(blocks, axis_name, split_axis=0, concat_axis=0, tiled=True)  49.5 us
    all_gather x1, blocking collectives, on_device(): all_rows = lax.all_gather(line_share, 'dp', axis=0, tiled=True)  23.4 us
    all_to_all x1, blocking collectives, on_device(): lax.all_to_all(jnp.stack([projected] * lax.axis_size('dp')), 'dp', 0, 0)  14.6 us
    all_gather x1, blocking collectives, on_device(): line_fresh = lax.all_gather(fresh, 'x', axis=0, tiled=True)  12.4 us
    dot_general x2, matrix products, expert_units(): return jnp.dot(active, units[2], preferred_element_type=F32).astype(BF16)  11.1 us
    dot_general x2, matrix products, contract_rows(): lax.dot_general(left_rows, unit_rows, (((1,), (1,)), ((), ())), preferred...  6.75 us
  transfers between devices with their start and end apart: 9, of which 8 were waited for; matrix products, arithmetic and copies ran while one was open for 9% of the time, Pallas kernels for 0%

profile of v1, /device:TPU:8, one launch (start us, length us, event | category | flops | bytes accessed | tf_op | source)
XLA Modules:
  0.0 234.0 jit_solution(11913844897924331075)
XLA Ops:
  10.6 1.8 convolution_convert_fusion.1
  13.3 10.2 %all-to-all-start = ((bf16[32,16,1536]{2,1,0:T(8,128)(2,1)}), bf16[32,16,1536]{2,1,0:T(8,128)(2,1)S(1)}, u32[]{:S(2)}, u32[]{:S(2)}) async-start(bf16[32,16,1536]{2,1,0:T(8,128)(2,1)} %bitcast.3), calls=%async_computation | async-start | bytes 3145728 | tf_op jit(solution)/shard_map/all_to_all | solution.py:19
  23.6 12.4 %all-gather = bf16[4,1,2048]{2,1,0:T(2,128)(2,1)S(1)} all-gather(bf16[1,1,2048]{2,1,0:T(2,128)(2,1)S(1)} %bitcast.121), channel_id=1, replica_groups=mesh['dp'=16,'y'=8,'x'=4] {'x'}, dimensions={0}, use_global_device_ids=true | all-gather | bytes 20480 | tf_op jit(solution)/shard_map/all_gather | solution.py:112
  36.0 23.4 %all-gather.1 = bf16[16,4,512]{2,1,0:T(4,128)(2,1)S(1)} all-gather(bf16[1,4,512]{2,1,0:T(4,128)(2,1)S(1)} %bitcast.123), channel_id=1, replica_groups=mesh['dp'=16,'y'=8,'x'=4] {'dp'}, dimensions={0}, use_global_device_ids=true | all-gather | bytes 69632 | tf_op jit(solution)/shard_map/all_gather | solution.py:114
  61.9 8.0 %all-to-all-start.1 = ((bf16[8,32,512]{2,1,0:T(8,128)(2,1)}), bf16[8,32,512]{2,1,0:T(8,128)(2,1)S(1)}, u32[]{:S(2)}, u32[]{:S(2)}) async-start(bf16[8,32,512]{2,1,0:T(8,128)(2,1)} %bitcast.4), calls=%async_computation.1 | async-start | bytes 524288 | tf_op jit(solution)/shard_map/all_to_all | solution.py:19
  69.9 10.9 %all-to-all-done.1 = bf16[8,32,512]{2,1,0:T(8,128)(2,1)S(1)} async-done(((bf16[8,32,512]{2,1,0:T(8,128)(2,1)}), bf16[8,32,512]{2,1,0:T(8,128)(2,1)S(1)}, u32[]{:S(2)}, u32[]{:S(2)}) %all-to-all-start.1) | async-done | bytes 262176 | tf_op jit(solution)/shard_map/all_to_all | solution.py:19
  81.7 3.3 %all-to-all-start.2 = ((bf16[4,32,512]{2,1,0:T(8,128)(2,1)}), bf16[4,32,512]{2,1,0:T(8,128)(2,1)S(1)}, u32[]{:S(2)}, u32[]{:S(2)}) async-start(bf16[4,32,512]{2,1,0:T(8,128)(2,1)} %bitcast.6), calls=%async_computation.2 | async-start | bytes 262144 | tf_op jit(solution)/shard_map/all_to_all | solution.py:19
  85.3 5.7 %all-to-all-done.2 = bf16[4,32,512]{2,1,0:T(8,128)(2,1)S(1)} async-done(((bf16[4,32,512]{2,1,0:T(8,128)(2,1)}), bf16[4,32,512]{2,1,0:T(8,128)(2,1)S(1)}, u32[]{:S(2)}, u32[]{:S(2)}) %all-to-all-start.2) | async-done | bytes 131104 | tf_op jit(solution)/shard_map/all_to_all | solution.py:19
  92.6 1.7 fusion.12
  95.6 5.0 %all-to-all-start.3 = ((bf16[32,16,128]{2,1,0:T(8,128)(2,1)}), bf16[32,16,128]{2,1,0:T(8,128)(2,1)S(1)}, u32[]{:S(2)}, u32[]{:S(2)}) async-start(bf16[32,16,128]{2,1,0:T(8,128)(2,1)} %copy.83), calls=%async_computation.3 | async-start | bytes 262144 | tf_op jit(solution)/shard_map/all_to_all | solution.py:19
  100.6 4.3 %fusion.5 = f32[512,768]{1,0:T(8,128)} fusion(bf16[512,1536]{1,0:T(8,128)(2,1)S(1)} %bitcast.107, bf16[3,768,1536]{2,1,0:T(8,128)(2,1)} %all-gather.4.cloned.1.call-done), kind=kOutput, calls=%fused_computation.14 | convolution fusion | flops 1207959552 | bytes 5505024 | tf_op jit(solution)/shard_map/dot_general | solution.py:13
  104.9 5.3 %all-to-all-done.3 = bf16[32,16,128]{2,1,0:T(8,128)(2,1)S(1)} async-done(((bf16[32,16,128]{2,1,0:T(8,128)(2,1)}), bf16[32,16,128]{2,1,0:T(8,128)(2,1)S(1)}, u32[]{:S(2)}, u32[]{:S(2)}) %all-to-all-start.3) | async-done | bytes 131104 | tf_op jit(solution)/shard_map/all_to_all | solution.py:19
  111.4 4.7 %all-to-all-start.4 = ((bf16[32,24,128]{2,1,0:T(8,128)(2,1)}), bf16[32,24,128]{2,1,0:T(8,128)(2,1)S(1)}, u32[]{:S(2)}, u32[]{:S(2)}) async-start(bf16[32,24,128]{2,1,0:T(8,128)(2,1)} %broadcast_in_dim.147), calls=%async_computation.4 | async-start | bytes 393216 | tf_op jit(solution)/shard_map/all_to_all | solution.py:19
  116.1 7.2 %convolution_convert_fusion = bf16[512,1536]{1,0:T(8,128)(2,1)} fusion(bf16[3,768,1536]{2,1,0:T(8,128)(2,1)} %all-gather.4.cloned.1.call-done, f32[512,768]{1,0:T(8,128)} %fusion.5, bf16[512,1536]{1,0:T(8,128)(2,1)S(1)} %bitcast.108), kind=kOutput, calls=%fused_computation | convolution fusion | flops 2417885184 | bytes 9437184 | tf_op jit(solution)/shard_map/dot_general | solution.py:48
  123.4 3.1 %all-to-all-done.4 = bf16[32,24,128]{2,1,0:T(8,128)(2,1)S(1)} async-done(((bf16[32,24,128]{2,1,0:T(8,128)(2,1)}), bf16[32,24,128]{2,1,0:T(8,128)(2,1)S(1)}, u32[]{:S(2)}, u32[]{:S(2)}) %all-to-all-start.4) | async-done | bytes 196640 | tf_op jit(solution)/shard_map/all_to_all | solution.py:19
  126.9 14.6 %all_to_all.45 = bf16[16,2,768]{2,1,0:T(2,128)(2,1)S(1)} all-to-all(bf16[16,2,768]{2,1,0:T(2,128)(2,1)S(1)} %reshape.265), channel_id=1, replica_groups=mesh['dp'=16,'y'=8,'x'=4] {'dp'}, dimensions={0} | all-to-all | bytes 98304 | tf_op jit(solution)/shard_map/all_to_all | solution.py:177
  141.4 7.0 %all-to-all-start.6 = ((bf16[32,16,1536]{2,1,0:T(8,128)(2,1)}), bf16[32,16,1536]{2,1,0:T(8,128)(2,1)S(1)}, u32[]{:S(2)}, u32[]{:S(2)}) async-start(bf16[32,16,1536]{2,1,0:T(8,128)(2,1)} %bitcast.21), calls=%async_computation.6 | async-start | bytes 3145728 | tf_op jit(solution)/shard_map/all_to_all | solution.py:19
  149.0 38.1 %all-to-all-done.6 = bf16[32,16,1536]{2,1,0:T(8,128)(2,1)S(1)} async-done(((bf16[32,16,1536]{2,1,0:T(8,128)(2,1)}), bf16[32,16,1536]{2,1,0:T(8,128)(2,1)S(1)}, u32[]{:S(2)}, u32[]{:S(2)}) %all-to-all-start.6) | async-done | bytes 1572896 | tf_op jit(solution)/shard_map/all_to_all | solution.py:19
  187.9 6.5 %all-to-all-start.7 = ((bf16[32,12,128]{2,1,0:T(8,128)(2,1)}), bf16[32,12,128]{2,1,0:T(8,128)(2,1)S(1)}, u32[]{:S(2)}, u32[]{:S(2)}) async-start(bf16[32,12,128]{2,1,0:T(8,128)(2,1)} %broadcast_in_dim.151), calls=%async_computation.7 | async-start | bytes 262144 | tf_op jit(solution)/shard_map/all_to_all | solution.py:19
  195.3 8.7 %all-to-all-done.7 = bf16[32,12,128]{2,1,0:T(8,128)(2,1)S(1)} async-done(((bf16[32,12,128]{2,1,0:T(8,128)(2,1)}), bf16[32,12,128]{2,1,0:T(8,128)(2,1)S(1)}, u32[]{:S(2)}, u32[]{:S(2)}) %all-to-all-start.7) | async-done | bytes 98336 | tf_op jit(solution)/shard_map/all_to_all | solution.py:19
  204.8 2.4 %fusion.10 = f32[32,768]{1,0:T(8,128)S(1)} fusion(bf16[3,768,1536]{2,1,0:T(8,128)(2,1)} %all-gather.4.cloned.1.call-done, bf16[32,1536]{1,0:T(8,128)(2,1)S(1)} %get-tuple-element.35, f32[1536]{0:T(1024)S(1)} %copy-done.5, f32[32]{0:T(128)S(1)} %add_rsqrt_fusion), kind=kOutput, calls=%fused_computation.23 | convolution fusion | flops 75718656 | bytes 2562176 | tf_op jit(solution)/shard_map/dot_general | solution.py:13
  207.3 3.9 %convolution_convert_fusion.2 = bf16[32,1536]{1,0:T(8,128)(2,1)S(1)} fusion(bf16[3,768,1536]{2,1,0:T(8,128)(2,1)} %all-gather.4.cloned.1.call-done, f32[32,768]{1,0:T(8,128)S(1)} %fusion.10, bf16[32,1536]{1,0:T(8,128)(2,1)S(1)} %get-tuple-element.35, f32[1536]{0:T(1024)S(1)} %copy-done.5, f32[32]{0:T(128)S(1)} %add_rsqrt_fusion), kind=kOutput, calls=%fused_computation.12 | convolution fusion | flops 151289856 | bytes 5019776 | tf_op jit(solution)/shard_map/dot_general | solution.py:48
  212.0 4.8 %all-to-all-start.8 = ((bf16[32,12,128]{2,1,0:T(8,128)(2,1)}), bf16[32,12,128]{2,1,0:T(8,128)(2,1)S(1)}, u32[]{:S(2)}, u32[]{:S(2)}) async-start(bf16[32,12,128]{2,1,0:T(8,128)(2,1)} %reshape.251), calls=%async_computation.8 | async-start | bytes 262144 | tf_op jit(solution)/shard_map/all_to_all | solution.py:19
  218.0 8.5 %all-to-all-done.8 = bf16[32,12,128]{2,1,0:T(8,128)(2,1)S(1)} async-done(((bf16[32,12,128]{2,1,0:T(8,128)(2,1)}), bf16[32,12,128]{2,1,0:T(8,128)(2,1)S(1)}, u32[]{:S(2)}, u32[]{:S(2)}) %all-to-all-start.8) | async-done | bytes 98336 | tf_op jit(solution)/shard_map/all_to_all | solution.py:19
  (120 shorter events, 18.0 us)
Async XLA Ops:
  7.2 119.3 %copy-start = (bf16[1536,48]{0,1:T(8,128)(2,1)S(1)}, bf16[1536,48]{0,1:T(8,128)(2,1)}, u32[]{:S(2)}) copy-start(bf16[1536,48]{0,1:T(8,128)(2,1)} %param.24) | copy-start | bytes 442372
  7.2 5.2 %copy-start.4 = (bf16[1,48,1536]{2,1,0:T(8,128)(2,1)S(1)}, bf16[1,48,1536]{2,1,0:T(8,128)(2,1)}, u32[]{:S(2)}) copy-start(bf16[1,48,1536]{2,1,0:T(8,128)(2,1)} %param.29) | copy-start | bytes 442372
  7.2 5.2 %copy-start.3 = (bf16[1,48,1536]{2,1,0:T(8,128)(2,1)S(1)}, bf16[1,48,1536]{2,1,0:T(8,128)(2,1)}, u32[]{:S(2)}) copy-start(bf16[1,48,1536]{2,1,0:T(8,128)(2,1)} %param.30) | copy-start | bytes 442372
  7.2 5.2 %copy-start.2 = (bf16[1,48,1536]{2,1,0:T(8,128)(2,1)S(1)}, bf16[1,48,1536]{2,1,0:T(8,128)(2,1)}, u32[]{:S(2)}) copy-start(bf16[1,48,1536]{2,1,0:T(8,128)(2,1)} %param.31) | copy-start | bytes 442372
  7.2 93.4 %all-gather.4.cloned.1.call-start = ((), (), s32[]{:S(2)}) async-start(), calls=%async_computation.9 | async-start | bytes 7520256 | tf_op jit(solution)/shard_map/all_gather | solution.py:105
  10.6 2.7 %copy-start.8 = (bf16[1,1536]{1,0:T(2,128)(2,1)S(1)}, bf16[1,1536]{1,0:T(2,128)(2,1)}, u32[]{:S(2)}) copy-start(bf16[1,1536]{1,0:T(2,128)(2,1)} %param.16) | copy-start | bytes 9220
  10.6 2.7 %copy-start.10 = (bf16[1,512]{1,0:T(2,128)(2,1)S(1)}, bf16[1,512]{1,0:T(2,128)(2,1)}, u32[]{:S(2)}) copy-start(bf16[1,512]{1,0:T(2,128)(2,1)} %param.17) | copy-start | bytes 3076
  13.3 46.1 %copy-start.14 = (s32[512]{0:T(512)S(1)}, s32[512]{0:T(512)}, u32[]{:S(2)}) copy-start(s32[512]{0:T(512)} %param.19) | copy-start | bytes 6148
  13.3 48.6 %all-to-all-start = ((bf16[32,16,1536]{2,1,0:T(8,128)(2,1)}), bf16[32,16,1536]{2,1,0:T(8,128)(2,1)S(1)}, u32[]{:S(2)}, u32[]{:S(2)}) async-start(bf16[32,16,1536]{2,1,0:T(8,128)(2,1)} %bitcast.3), calls=%async_computation | async-start | bytes 3145728 | tf_op jit(solution)/shard_map/all_to_all | solution.py:19
  23.5 61.5 %copy-start.11 = (s32[32]{0:T(128)S(1)}, s32[32]{0:T(128)}, u32[]{:S(2)}) copy-start(s32[32]{0:T(128)} %param.20) | copy-start | bytes 388
  23.5 61.5 %copy-start.12 = (s32[32]{0:T(128)S(1)}, s32[32]{0:T(128)}, u32[]{:S(2)}) copy-start(s32[32]{0:T(128)} %param.21) | copy-start | bytes 388
  23.5 61.7 %copy-start.9 = (bf16[1,1536]{1,0:T(2,128)(2,1)S(1)}, bf16[1,1536]{1,0:T(2,128)(2,1)}, u32[]{:S(2)}) copy-start(bf16[1,1536]{1,0:T(2,128)(2,1)} %param.18) | copy-start | bytes 9220
  23.6 67.5 %copy-start.13 = (bf16[32,2,64,128]{3,2,1,0:T(8,128)(2,1)S(1)}, bf16[32,2,64,128]{3,2,1,0:T(8,128)(2,1)}, u32[]{:S(2)}) copy-start(bf16[32,2,64,128]{3,2,1,0:T(8,128)(2,1)} %param.22) | copy-start | bytes 3145732
  61.9 18.9 %all-to-all-start.1 = ((bf16[8,32,512]{2,1,0:T(8,128)(2,1)}), bf16[8,32,512]{2,1,0:T(8,128)(2,1)S(1)}, u32[]{:S(2)}, u32[]{:S(2)}) async-start(bf16[8,32,512]{2,1,0:T(8,128)(2,1)} %bitcast.4), calls=%async_computation.1 | async-start | bytes 524288 | tf_op jit(solution)/shard_map/all_to_all | solution.py:19
  81.7 9.3 %all-to-all-start.2 = ((bf16[4,32,512]{2,1,0:T(8,128)(2,1)}), bf16[4,32,512]{2,1,0:T(8,128)(2,1)S(1)}, u32[]{:S(2)}, u32[]{:S(2)}) async-start(bf16[4,32,512]{2,1,0:T(8,128)(2,1)} %bitcast.6), calls=%async_computation.2 | async-start | bytes 262144 | tf_op jit(solution)/shard_map/all_to_all | solution.py:19
  95.6 14.6 %all-to-all-start.3 = ((bf16[32,16,128]{2,1,0:T(8,128)(2,1)}), bf16[32,16,128]{2,1,0:T(8,128)(2,1)S(1)}, u32[]{:S(2)}, u32[]{:S(2)}) async-start(bf16[32,16,128]{2,1,0:T(8,128)(2,1)} %copy.83), calls=%async_computation.3 | async-start | bytes 262144 | tf_op jit(solution)/shard_map/all_to_all | solution.py:19
  111.4 15.0 %all-to-all-start.4 = ((bf16[32,24,128]{2,1,0:T(8,128)(2,1)}), bf16[32,24,128]{2,1,0:T(8,128)(2,1)S(1)}, u32[]{:S(2)}, u32[]{:S(2)}) async-start(bf16[32,24,128]{2,1,0:T(8,128)(2,1)} %broadcast_in_dim.147), calls=%async_computation.4 | async-start | bytes 393216 | tf_op jit(solution)/shard_map/all_to_all | solution.py:19
  141.4 7.0 %copy-start.7 = (f32[64,4]{0,1:T(4,128)S(1)}, f32[64,4]{0,1:T(4,128)}, u32[]{:S(2)}) copy-start(f32[64,4]{0,1:T(4,128)} %param.27) | copy-start | bytes 3076
  141.4 7.0 %copy-start.6 = (s32[64,4]{0,1:T(4,128)S(1)}, s32[64,4]{0,1:T(4,128)}, u32[]{:S(2)}) copy-start(s32[64,4]{0,1:T(4,128)} %param.26) | copy-start | bytes 3076
  141.4 45.7 %all-to-all-start.6 = ((bf16[32,16,1536]{2,1,0:T(8,128)(2,1)}), bf16[32,16,1536]{2,1,0:T(8,128)(2,1)S(1)}, u32[]{:S(2)}, u32[]{:S(2)}) async-start(bf16[32,16,1536]{2,1,0:T(8,128)(2,1)} %bitcast.21), calls=%async_computation.6 | async-start | bytes 3145728 | tf_op jit(solution)/shard_map/all_to_all | solution.py:19
  187.9 16.0 %all-to-all-start.7 = ((bf16[32,12,128]{2,1,0:T(8,128)(2,1)}), bf16[32,12,128]{2,1,0:T(8,128)(2,1)S(1)}, u32[]{:S(2)}, u32[]{:S(2)}) async-start(bf16[32,12,128]{2,1,0:T(8,128)(2,1)} %broadcast_in_dim.151), calls=%async_computation.7 | async-start | bytes 262144 | tf_op jit(solution)/shard_map/all_to_all | solution.py:19
  194.8 10.0 %copy-start.5 = (f32[1536]{0:T(1024)S(1)}, f32[1536]{0:T(1024)}, u32[]{:S(2)}) copy-start(f32[1536]{0:T(1024)} %param.28) | copy-start | bytes 18436
  207.3 9.5 %copy-start.1 = (bf16[63,1536]{1,0:T(8,128)(2,1)S(1)}, bf16[63,1536]{1,0:T(8,128)(2,1)}, u32[]{:S(2)}) copy-start(bf16[63,1536]{1,0:T(8,128)(2,1)} %param.25) | copy-start | bytes 580612
  212.0 14.5 %all-to-all-start.8 = ((bf16[32,12,128]{2,1,0:T(8,128)(2,1)}), bf16[32,12,128]{2,1,0:T(8,128)(2,1)S(1)}, u32[]{:S(2)}, u32[]{:S(2)}) async-start(bf16[32,12,128]{2,1,0:T(8,128)(2,1)} %reshape.251), calls=%async_computation.8 | async-start | bytes 262144 | tf_op jit(solution)/shard_map/all_to_all | solution.py:19
Sparse Core Ops, SparseCore 0:
  13.4 58.0 all-gather.3
